TPU v7x, 512 devices: a whole 4x4x16 slice. The times are simulated.
512 devices in a mesh: rows: 128 (over y, z, core), users: 4 (over x).
Axes of the slice: x: 4, y: 4, z: 16, core: 2. Of those that a mesh axis runs over, the one named last changes fastest.
Arguments:
- old_basis: bfloat16 [49152, 4096], P('rows', 'users'), may hold values from -24 to 24
- new_atoms: bfloat16 [49152, 128], P('rows'), may hold values from -300 to 300
- user_residuals: bfloat16 [49152, 512], P('rows', 'users'), may hold values from -850 to 850
Outputs:
- new_block: bfloat16 [49152, 128], P('rows')
- updated_residuals: bfloat16 [49152, 512], P('rows', 'users')
All inputs are finite; a program needn't handle non-finite values.
Results may differ from a plain program's by a relative error of at most 0.019.
Values may be sent and summed in bfloat16 or wider, within the bound.
A program may use at most 64 MiB of HBM per device.

v0:
```python
import jax
import jax.numpy as jnp
from jax import lax
from jax.sharding import PartitionSpec as P


def coefficient_sum(partial_coef, m_total):
    summed = lax.psum(partial_coef, "rows")
    return (summed / m_total).astype(jnp.bfloat16)


def rows_product(left_rows, right_rows):
    return jnp.einsum("rk,rb->kb", left_rows, right_rows, preferred_element_type=jnp.float32)


def finish_block(remainder_low, gram_total, coupling_total, user_residuals, m_total):
    gram_matrix = gram_total / m_total
    factor_lower = jnp.linalg.cholesky(gram_matrix)
    identity = jnp.eye(gram_matrix.shape[0], dtype=jnp.float32)
    inverse = jax.scipy.linalg.solve_triangular(factor_lower, identity, lower=True)
    new_block = jnp.dot(
        remainder_low.astype(jnp.float32), inverse.T, precision=lax.Precision.HIGHEST
    ).astype(jnp.bfloat16)
    weights_low = jnp.dot(
        inverse, coupling_total / m_total, precision=lax.Precision.HIGHEST
    ).astype(jnp.bfloat16)
    updated = user_residuals.astype(jnp.float32) - jnp.dot(
        new_block, weights_low, preferred_element_type=jnp.float32
    )
    return (new_block, updated.astype(jnp.bfloat16))


def local(old_basis, new_atoms, user_residuals):
    local_rows = old_basis.shape[0]
    m_total = float(local_rows * lax.axis_size("rows"))
    remainder = new_atoms.astype(jnp.float32)
    remainder_low = new_atoms
    for sweep_index in range(2):
        coef_low = coefficient_sum(rows_product(old_basis, remainder_low), m_total)
        local_image = jnp.dot(old_basis, coef_low, preferred_element_type=jnp.float32)
        projected = lax.psum(local_image, "users")
        remainder = remainder - projected
        remainder_low = remainder.astype(jnp.bfloat16)
    gram_total, coupling_total = lax.psum(
        (rows_product(remainder_low, remainder_low), rows_product(remainder_low, user_residuals)),
        "rows",
    )
    return finish_block(remainder_low, gram_total, coupling_total, user_residuals, m_total)


def solution(mesh):
    in_specs = (P("rows", "users"), P("rows", None), P("rows", "users"))
    out_specs = (P("rows", None), P("rows", "users"))
    return jax.shard_map(local, mesh=mesh, in_specs=in_specs, out_specs=out_specs, check_vma=False)
```

profile of v0, /device:TPU:1, one launch (start us, length us, event | category | flops | bytes accessed | tf_op | source)
XLA Modules:
  0.0 1167.1 jit_solution(7656072023004440981)
XLA Ops:
  7.2 0.0 copy-start
  7.2 0.0 all-reduce.7.cloned.1.call-start
  7.2 1.1 copy-done
  8.3 2.1 fusion.14
  10.4 0.0 all-reduce.7.cloned.1.call-update
  10.4 0.0 all-reduce.9.cloned.1.call-start
  10.5 341.4 %all-reduce.7.cloned.1.call-done = f32[1024,128]{1,0:T(8,128)} async-done(((f32[1024,128]{1,0:T(8,128)}), f32[1024,128]{1,0:T(8,128)}) %all-reduce.7.cloned.1.call-update) | async-done | bytes 524304 | tf_op jit(solution)/shard_map/psum | solution.py:8
  351.9 2.1 convolution_bitcast_fusion.2
  354.0 0.0 copy-start.4
  354.0 0.0 all-reduce.9.cloned.1.call-update
  354.0 0.0 all-reduce.11.cloned.1.call-start
  354.0 0.8 copy-done.4
  354.9 0.1 copy.5
  355.0 52.0 %all-reduce.9.cloned.1.call-done = f32[384,128]{0,1:T(8,128)} async-done(((f32[384,128]{0,1:T(8,128)}), f32[384,128]{0,1:T(8,128)}) %all-reduce.9.cloned.1.call-update) | async-done | bytes 196624 | tf_op jit(solution)/shard_map/psum | solution.py:41
  407.0 2.2 convolution_bitcast_fusion
  409.1 0.0 all-reduce.11.cloned.1.call-update
  409.2 0.0 all-reduce.13.cloned.1.call-start
  409.2 339.0 %all-reduce.11.cloned.1.call-done = f32[1024,128]{1,0:T(8,128)} async-done(((f32[1024,128]{1,0:T(8,128)}), f32[1024,128]{1,0:T(8,128)}) %all-reduce.11.cloned.1.call-update) | async-done | bytes 524304 | tf_op jit(solution)/shard_map/psum | solution.py:8
  748.2 2.1 convolution_bitcast_fusion.1
  750.3 0.0 copy-start.1
  750.3 0.0 all-reduce.13.cloned.1.call-update
  750.3 0.0 all-reduce.15.cloned.1.call-start
  750.4 52.9 %all-reduce.13.cloned.1.call-done = f32[384,128]{0,1:T(8,128)} async-done(((f32[384,128]{0,1:T(8,128)}), f32[384,128]{0,1:T(8,128)}) %all-reduce.13.cloned.1.call-update) | async-done | bytes 196624 | tf_op jit(solution)/shard_map/psum | solution.py:41
  803.2 0.0 copy-done.1
  803.2 1.0 subtract_convert_fusion
  804.2 0.0 copy-start.2
  804.2 0.8 fusion.15
  805.0 0.1 copy-done.2
  805.1 0.9 fusion.16
  805.9 0.0 all-reduce.15.cloned.1.call-update
  806.0 327.9 %all-reduce.15.cloned.1.call-done = (f32[128,128]{0,1:T(8,128)}, f32[128,128]{0,1:T(8,128)}) async-done(((f32[128,128]{0,1:T(8,128)}, f32[128,128]{0,1:T(8,128)}), (f32[128,128]{0,1:T(8,128)}, f32[128,128]{0,1:T(8,128)})) %all-reduce.15.cloned.1.call-update) | async-done | bytes 131088 | tf_op jit(solution)/shard_map/psum | solution.py:44
  1133.8 0.8 broadcast_multiply_fusion
  1134.7 0.0 copy-start.5
  1134.7 0.1 copy.7
  1134.8 0.7 copy-done.5
  1135.5 11.7 %cholesky.17 = f32[128,128]{1,0:T(8,128)S(1)} custom-call(f32[128,128]{1,0:T(8,128)S(1)} %fusion.8), custom_call_target="Cholesky" | custom-call | tf_op jit(solution)/shard_map/jit(cholesky)/cholesky | solution.py:18
  1147.3 0.6 compare_reduce_fusion
  1147.9 0.7 fusion.5
  1148.6 9.8 custom-call.7
  1158.4 0.2 fusion.6
  1158.7 0.0 copy-start.6
  1158.7 0.3 convolution_convert_fusion
  1159.0 0.0 copy-start.3
  1159.0 0.5 copy-done.6
  1159.5 0.3 convolution_convert_fusion.1
  1159.8 0.8 fusion
  1160.6 0.0 copy-done.3
  (2 shorter events, 0.0 us)
Async XLA Ops:
  7.2 1.1 copy-start
  7.2 344.7 %all-reduce.7.cloned.1.call-start = ((), (), s32[]{:S(2)}) async-start(), calls=%async_computation | async-start | bytes 1048576 | tf_op jit(solution)/shard_map/psum | solution.py:8
  10.4 396.6 %all-reduce.9.cloned.1.call-start = ((), (), s32[]{:S(2)}) async-start(), calls=%async_computation.1 | async-start | bytes 393216 | tf_op jit(solution)/shard_map/psum | solution.py:41
  354.0 0.9 copy-start.4
  354.0 394.2 %all-reduce.11.cloned.1.call-start = ((), (), s32[]{:S(2)}) async-start(), calls=%async_computation.2 | async-start | bytes 1048576 | tf_op jit(solution)/shard_map/psum | solution.py:8
  409.2 394.1 %all-reduce.13.cloned.1.call-start = ((), (), s32[]{:S(2)}) async-start(), calls=%async_computation.3 | async-start | bytes 393216 | tf_op jit(solution)/shard_map/psum | solution.py:41
  750.3 52.9 %copy-start.1 = (f32[384,128]{0,1:T(8,128)S(1)}, f32[384,128]{0,1:T(8,128)}, u32[]{:S(2)}) copy-start(f32[384,128]{0,1:T(8,128)} %all-reduce.9.cloned.1.call-done) | copy-start | bytes 589828
  750.3 383.5 %all-reduce.15.cloned.1.call-start = ((), (), s32[]{:S(2)}) async-start(), calls=%async_computation.4 | async-start | bytes 262144 | tf_op jit(solution)/shard_map/psum | solution.py:44
  804.2 0.9 copy-start.2
  1134.7 0.8 copy-start.5
  1158.7 0.8 copy-start.6
  1159.0 1.6 copy-start.3
Sparse Core Ops, SparseCore 0:
  11.4 340.3 all-reduce.6
  354.2 52.7 all-reduce.8
  410.4 337.7 all-reduce.10
  750.5 52.7 all-reduce.12
  807.2 326.6 all-reduce.14
where the time goes:
time: 1170 us
  waiting for transfers between devices  1110 us (95%)
  other arithmetic  24.7 us (2%)
  between operations  13.9 us (1%)
    psum x2, waiting for transfers between devices, coefficient_sum(): summed = lax.psum(partial_coef, 'rows')  680 us
    psum x1, waiting for transfers between devices, local(): lax.psum((rows_product(remainder_low, remainder_low), rows_product(remain...  328 us
    psum x2, waiting for transfers between devices, local(): projected = lax.psum(local_image, 'users')  105 us
  transfers between devices with their start and end apart: 5, of which 5 were waited for; matrix products, arithmetic and copies ran while one was open for 0% of the time, Pallas kernels for 0%

commit v1 on v0

v1 whole, which is shorter than its diff:
```python
import functools

import jax
import jax.numpy as jnp
from jax import lax
from jax.experimental import pallas as pl
from jax.experimental.pallas import tpu as pltpu
from jax.sharding import PartitionSpec as P

MESH = pl.DeviceIdType.MESH
F32 = jnp.float32
BF16 = jnp.bfloat16
Y, Z, CORES, X = 4, 16, 2, 4
STRIPE = 2
ROW_CHUNKS = 3


def place():
    row = lax.axis_index("rows")
    z = lax.rem(lax.div(row, CORES), Z)
    return (
        lax.div(row, CORES * Z),
        lax.div(z, STRIPE),
        lax.rem(z, STRIPE),
        lax.rem(row, CORES),
        lax.axis_index("users"),
    )


def device(y, pair, stripe, core, x):
    return ((y * Z + pair * STRIPE + stripe) * CORES + core, x)


def half_of(pair, stripe, core):
    pairs = Z // STRIPE
    return lax.rem(core + stripe + lax.div(2 * pair, pairs), 2)


def core_of(pair, stripe, half):
    pairs = Z // STRIPE
    return lax.rem(half + stripe + lax.div(2 * pair, pairs), 2)


def ring_order(n):
    return sorted(range(1, n), key=lambda d: -min(d, n - d))


def exchange_kernel(
    m_total,
    basis_hbm, atoms_hbm, users_hbm,
    low_out, sums_out,
    basis, atoms, users, low, remainder,
    mate_out, mate_in, patch_out, patch_in, far_out, far_in, own_piece, coef, image, own_image,
    gram_out, gram_in, gpatch_out, gpatch_in, gfar_in, gown, gpiece,
    load_sem,
    mate_s, mate_r, patch_s, patch_r, far_s, far_r, gather_s, gather_r, users_s, users_r,
):
    y, pair, stripe, core, x = place()
    pairs = Z // STRIPE
    owners = Y * STRIPE
    half = half_of(pair, stripe, core)
    owner = y * STRIPE + stripe
    atoms_b = atoms.shape[1]
    side = atoms_b // 2
    piece_rows = side // Y
    k_loc = basis.shape[1]
    piece_cols = k_loc // STRIPE
    rows = basis.shape[0]
    chunk = rows // ROW_CHUNKS
    gram_rows = side // owners

    def patch_device(shift):
        other = lax.rem(owner + shift, owners)
        other_y, other_stripe = lax.div(other, STRIPE), lax.rem(other, STRIPE)
        return other, other_y, other_stripe

    def same_half(shift):
        other, other_y, other_stripe = patch_device(shift)
        return device(other_y, pair, other_stripe, core_of(pair, other_stripe, half), x)

    def other_half(shift):
        other, other_y, other_stripe = patch_device(shift)
        return device(other_y, pair, other_stripe, core_of(pair, other_stripe, 1 - half), x)

    def far_device(shift):
        other = lax.rem(pair + shift, pairs)
        return device(y, other, stripe, core_of(other, stripe, half), x)

    def user_device(shift):
        return device(y, pair, stripe, core, lax.rem(x + shift, X))

    mate = device(y, pair, stripe, 1 - core, x)
    patch_order = sorted(range(1, owners), key=lambda d: -min(d, owners - d))
    far_order = ring_order(pairs)
    user_order = ring_order(X)

    barrier = pltpu.get_barrier_semaphore()
    peers = [mate]
    peers += [same_half(d) for d in patch_order] + [other_half(d) for d in patch_order]
    peers += [far_device(d) for d in far_order] + [user_device(d) for d in user_order]
    for peer in peers:
        pl.semaphore_signal(barrier, inc=1, device_id=peer, device_id_type=MESH)

    loads = [
        pltpu.make_async_copy(atoms_hbm, atoms, load_sem.at[0]),
        pltpu.make_async_copy(basis_hbm, basis, load_sem.at[1]),
        pltpu.make_async_copy(users_hbm, users, load_sem.at[2]),
    ]
    for load in loads:
        load.start()
    loads[0].wait()
    low[...] = atoms[...]
    remainder[...] = atoms[...].astype(F32)
    loads[1].wait()
    loads[2].wait()
    pl.semaphore_wait(barrier, len(peers))

    def remote(src, dst, send, recv, peer):
        return pltpu.make_async_remote_copy(
            src_ref=src, dst_ref=dst, send_sem=send, recv_sem=recv, device_id=peer, device_id_type=MESH
        )

    for sweep in range(2):
        sent = []
        turned = low[...].astype(F32).T.astype(BF16)
        halves = []
        mates = []
        for s in range(STRIPE):
            cols = pl.ds(s * piece_cols, piece_cols)
            product = jnp.dot(turned, basis[:, cols], preferred_element_type=F32)
            own_piece[:, cols] = product
            mate_out[sweep, :, cols] = own_piece[pl.ds(pl.multiple_of((1 - half) * side, side), side), cols].astype(BF16)
            copy = remote(
                mate_out.at[sweep, :, cols], mate_in.at[sweep, :, cols],
                mate_s.at[sweep, s], mate_r.at[sweep, s], mate,
            )
            copy.start()
            mates.append(copy)
        sent += mates
        for s in range(STRIPE):
            cols = pl.ds(s * piece_cols, piece_cols)
            mates[s].wait_recv()
            total = own_piece[pl.ds(pl.multiple_of(half * side, side), side), cols] + mate_in[sweep, :, cols].astype(F32)
            patch_out[sweep, :, cols] = total.astype(BF16)
        patch_copies = []
        for i, d in enumerate(patch_order):
            other, other_y, other_stripe = patch_device(d)
            src = patch_out.at[
                sweep,
                pl.ds(pl.multiple_of(other_y * piece_rows, piece_rows), piece_rows),
                pl.ds(pl.multiple_of(other_stripe * piece_cols, piece_cols), piece_cols),
            ]
            copy = remote(src, patch_in.at[sweep, owner], patch_s.at[sweep, i], patch_r.at[sweep, i], same_half(d))
            copy.start()
            patch_copies.append(copy)
        patch_in[sweep, owner] = patch_out[
            sweep,
            pl.ds(pl.multiple_of(y * piece_rows, piece_rows), piece_rows),
            pl.ds(pl.multiple_of(stripe * piece_cols, piece_cols), piece_cols),
        ]
        for copy in patch_copies:
            copy.wait_recv()
        sent += patch_copies
        total = patch_in[sweep, 0].astype(F32)
        for j in range(1, owners):
            total = total + patch_in[sweep, j].astype(F32)
        far_out[sweep] = total.astype(BF16)
        far_copies = []
        for i, d in enumerate(far_order):
            copy = remote(far_out.at[sweep], far_in.at[sweep, pair], far_s.at[sweep, i], far_r.at[sweep, i], far_device(d))
            copy.start()
            far_copies.append(copy)
        far_in[sweep, pair] = far_out[sweep]
        for copy in far_copies:
            copy.wait_recv()
        sent += far_copies
        total = far_in[sweep, 0].astype(F32)
        for j in range(1, pairs):
            total = total + far_in[sweep, j].astype(F32)
        mine = coef.at[
            sweep,
            pl.ds(pl.multiple_of(half * side + y * piece_rows, piece_rows), piece_rows),
            pl.ds(pl.multiple_of(stripe * piece_cols, piece_cols), piece_cols),
        ]
        mine[...] = (total / m_total).astype(BF16)
        gathers = []
        for i, d in enumerate(patch_order):
            for j, target in enumerate((same_half(d), other_half(d))):
                copy = remote(mine, mine, gather_s.at[sweep, 2 * i + j], gather_r.at[sweep, 2 * i + j], target)
                copy.start()
                gathers.append(copy)
        copy = remote(mine, mine, gather_s.at[sweep, 2 * owners - 2], gather_r.at[sweep, 2 * owners - 2], mate)
        copy.start()
        gathers.append(copy)
        for copy in gathers:
            copy.wait_recv()
        sent += gathers

        user_copies = []
        for c in range(ROW_CHUNKS):
            part = pl.ds(c * chunk, chunk)
            product = lax.dot_general(
                basis[part, :], coef[sweep], (((1,), (1,)), ((), ())), preferred_element_type=F32
            )
            own_image[sweep, part, :] = product.astype(BF16)
            for i, d in enumerate(user_order):
                copy = remote(
                    own_image.at[sweep, part, :], image.at[sweep, x, part, :],
                    users_s.at[sweep, c, i], users_r.at[sweep, c, i], user_device(d),
                )
                copy.start()
                user_copies.append(copy)
            image[sweep, x, part, :] = own_image[sweep, part, :]
        for c in range(ROW_CHUNKS):
            part = pl.ds(c * chunk, chunk)
            for copy in user_copies[c * len(user_order) : (c + 1) * len(user_order)]:
                copy.wait_recv()
            projected = image[sweep, 0, part, :].astype(F32)
            for j in range(1, X):
                projected = projected + image[sweep, j, part, :].astype(F32)
            left = remainder[part, :] - projected
            remainder[part, :] = left
            low[part, :] = left.astype(BF16)
        sent += user_copies
        for copy in sent:
            copy.wait_send()

    low_out[...] = low[...]
    turned = low[...].astype(F32).T.astype(BF16)
    gown[:, :atoms_b] = jnp.dot(turned, low[...], preferred_element_type=F32)
    gown[:, atoms_b:] = jnp.dot(turned, users[...], preferred_element_type=F32)
    gram_out[...] = gown[pl.ds(pl.multiple_of((1 - half) * side, side), side), :]
    sent = []
    copy = remote(gram_out, gram_in, mate_s.at[2, 0], mate_r.at[2, 0], mate)
    copy.start()
    sent.append(copy)
    copy.wait_recv()
    gpatch_out[...] = gown[pl.ds(pl.multiple_of(half * side, side), side), :] + gram_in[...]
    patch_copies = []
    for i, d in enumerate(patch_order):
        other, _, _ = patch_device(d)
        src = gpatch_out.at[pl.ds(pl.multiple_of(other * gram_rows, gram_rows), gram_rows), :]
        copy = remote(src, gpatch_in.at[owner], patch_s.at[2, i], patch_r.at[2, i], same_half(d))
        copy.start()
        patch_copies.append(copy)
    gpatch_in[owner] = gpatch_out[pl.ds(pl.multiple_of(owner * gram_rows, gram_rows), gram_rows), :]
    for copy in patch_copies:
        copy.wait_recv()
    sent += patch_copies
    total = gpatch_in[0]
    for j in range(1, owners):
        total = total + gpatch_in[j]
    gpiece[...] = total
    far_copies = []
    for i, d in enumerate(far_order):
        copy = remote(gpiece, gfar_in.at[pair], far_s.at[2, i], far_r.at[2, i], far_device(d))
        copy.start()
        far_copies.append(copy)
    gfar_in[pair] = gpiece[...]
    for copy in far_copies:
        copy.wait_recv()
    sent += far_copies
    total = gfar_in[0]
    for j in range(1, pairs):
        total = total + gfar_in[j]
    mine = sums_out.at[pl.ds(pl.multiple_of(half * side + owner * gram_rows, gram_rows), gram_rows), :]
    mine[...] = total / m_total
    gathers = []
    for i, d in enumerate(patch_order):
        for j, target in enumerate((same_half(d), other_half(d))):
            copy = remote(mine, mine, gather_s.at[2, 2 * i + j], gather_r.at[2, 2 * i + j], target)
            copy.start()
            gathers.append(copy)
    copy = remote(mine, mine, gather_s.at[2, 2 * owners - 2], gather_r.at[2, 2 * owners - 2], mate)
    copy.start()
    gathers.append(copy)
    for copy in gathers:
        copy.wait_recv()
    sent += gathers
    for copy in sent:
        copy.wait_send()


def exchange(old_basis, new_atoms, user_residuals, m_total):
    rows, k_loc = old_basis.shape
    b = new_atoms.shape[1]
    u = user_residuals.shape[1]
    owners, pairs = Y * STRIPE, Z // STRIPE
    side = b // 2
    piece = (side // Y, k_loc // STRIPE)
    gram_piece = (side // owners, b + u)
    dma = pltpu.SemaphoreType.DMA
    n_gather = 2 * owners - 1
    scratch = [
        pltpu.VMEM((rows, k_loc), BF16),
        pltpu.VMEM((rows, b), BF16),
        pltpu.VMEM((rows, u), BF16),
        pltpu.VMEM((rows, b), BF16),
        pltpu.VMEM((rows, b), F32),
        pltpu.VMEM((2, side, k_loc), BF16),
        pltpu.VMEM((2, side, k_loc), BF16),
        pltpu.VMEM((2, side, k_loc), BF16),
        pltpu.VMEM((2, owners, *piece), BF16),
        pltpu.VMEM((2, *piece), BF16),
        pltpu.VMEM((2, pairs, *piece), BF16),
        pltpu.VMEM((b, k_loc), F32),
        pltpu.VMEM((2, b, k_loc), BF16),
        pltpu.VMEM((2, X, rows, b), BF16),
        pltpu.VMEM((2, rows, b), BF16),
        pltpu.VMEM((side, b + u), F32),
        pltpu.VMEM((side, b + u), F32),
        pltpu.VMEM((side, b + u), F32),
        pltpu.VMEM((owners, *gram_piece), F32),
        pltpu.VMEM((pairs, *gram_piece), F32),
        pltpu.VMEM((b, b + u), F32),
        pltpu.VMEM(gram_piece, F32),
        dma((3,)),
        dma((3, STRIPE)), dma((3, STRIPE)),
        dma((3, max(owners - 1, 1))), dma((3, max(owners - 1, 1))),
        dma((3, max(pairs - 1, 1))), dma((3, max(pairs - 1, 1))),
        dma((3, n_gather)), dma((3, n_gather)),
        dma((2, ROW_CHUNKS, max(X - 1, 1))), dma((2, ROW_CHUNKS, max(X - 1, 1))),
    ]
    return pl.pallas_call(
        functools.partial(exchange_kernel, m_total),
        out_shape=(jax.ShapeDtypeStruct((rows, b), BF16), jax.ShapeDtypeStruct((b, b + u), F32)),
        in_specs=[pl.BlockSpec(memory_space=pl.ANY)] * 3,
        out_specs=(pl.BlockSpec(memory_space=pltpu.VMEM), pl.BlockSpec(memory_space=pltpu.VMEM)),
        scratch_shapes=scratch,
        compiler_params=pltpu.CompilerParams(collective_id=0, has_side_effects=True, vmem_limit_bytes=48 * 2**20),
    )(old_basis, new_atoms, user_residuals)


def finish_block(remainder_low, gram_matrix, coupling, user_residuals):
    factor_lower = jnp.linalg.cholesky(gram_matrix)
    identity = jnp.eye(gram_matrix.shape[0], dtype=F32)
    inverse = jax.scipy.linalg.solve_triangular(factor_lower, identity, lower=True)
    new_block = jnp.dot(remainder_low.astype(F32), inverse.T, precision=lax.Precision.HIGHEST).astype(BF16)
    weights_low = jnp.dot(inverse, coupling, precision=lax.Precision.HIGHEST).astype(BF16)
    updated = user_residuals.astype(F32) - jnp.dot(new_block, weights_low, preferred_element_type=F32)
    return (new_block, updated.astype(BF16))


def local(old_basis, new_atoms, user_residuals):
    m_total = float(old_basis.shape[0] * lax.axis_size("rows"))
    b = new_atoms.shape[1]
    remainder_low, sums = exchange(old_basis, new_atoms, user_residuals, m_total)
    return finish_block(remainder_low, sums[:, :b], sums[:, b:], user_residuals)


def solution(mesh):
    in_specs = (P("rows", "users"), P("rows", None), P("rows", "users"))
    out_specs = (P("rows", None), P("rows", "users"))
    return jax.shard_map(local, mesh=mesh, in_specs=in_specs, out_specs=out_specs, check_vma=False)
```

time: 1170 us -> 117 us (0.10)
  waiting for transfers between devices: 1110 us -> 0 us
  Pallas kernels: 0 us -> 88 us
  between operations: 13.9 us -> 0.72 us
    psum x5 -> x0, waiting for transfers between devices: 1110 us -> none  [the longest x2 680 us: coefficient_sum(): summed = lax.psum(partial_coef, 'rows')]
    pallas_call x0 -> x1, Pallas kernels: none -> 88 us  [exchange(): pl.pallas_call(functools.partial(exchange_kernel, m_total), out_shape=(ja...]
  transfers between devices with their start and end apart: 5 -> 0, of which waited for: 5 -> 0; matrix products, arithmetic and copies ran while one was open for 0% -> 0% of each run, Pallas kernels for 0% -> 0%
where the time goes in v1:
time: 117 us
  Pallas kernels  88 us (75%)
  other arithmetic  22.9 us (20%)
  local copies, waits for them, and re-layouts  3.72 us (3%)
  matrix products  1.52 us (1%)
    pallas_call x1, Pallas kernels, exchange(): pl.pallas_call(functools.partial(exchange_kernel, m_total), out_shape=(ja...  88 us
    another operation x3, other arithmetic, finish_block(): factor_lower = jnp.linalg.cholesky(gram_matrix)  12.4 us
    another operation x2, other arithmetic, finish_block(): jax.scipy.linalg.solve_triangular(factor_lower, identity, lower=True)  10.5 us
    unnamed x10, local copies, waits for them, and re-layouts  3.54 us

profile of v1, /device:TPU:1, one launch (start us, length us, event | category | flops | bytes accessed | tf_op | source)
XLA Modules:
  0.0 116.9 jit_solution(8360924240100705721)
XLA Ops:
  0.6 0.0 copy-start
  0.6 1.1 copy-done
  1.8 0.0 copy-start.1
  1.8 0.9 copy-done.1
  2.7 0.0 copy-start.3
  2.7 0.9 copy-done.3
  3.5 88.0 %shard_map.50 = (bf16[384,128]{1,0:T(8,128)(2,1)S(1)}, f32[128,256]{1,0:T(8,128)S(1)}) custom-call(bf16[384,1024]{1,0:T(8,128)(2,1)S(1)} %copy-done, bf16[384,128]{1,0:T(8,128)(2,1)S(1)} %copy-done.3, bf16[384,128]{1,0:T(8,128)(2,1)S(1)} %copy-done.1), custom_call_target="tpu_custom_call" | custom-call | tf_op jit(solution)/shard_map/pallas_call | solution.py:324
  91.6 0.1 copy.5
  91.7 0.1 copy.6
  91.8 11.7 %cholesky.17 = f32[128,128]{1,0:T(8,128)S(1)} custom-call(f32[128,128]{1,0:T(8,128)S(1)} %fusion.4), custom_call_target="Cholesky" | custom-call | tf_op jit(solution)/shard_map/jit(cholesky)/cholesky | solution.py:335
  103.6 0.6 compare_reduce_fusion
  104.2 0.7 fusion.1
  104.9 9.8 %custom-call.7 = f32[1,128,128]{1,2,0:T(8,128)S(1)} custom-call(f32[1,128,128]{2,1,0:T(8,128)S(1)} %fusion.1), custom_call_target="InvertDiagBlocksLowerTriangular" | custom-call | tf_op jit(solution)/shard_map/jit(_solve_triangular)/triangular_solve | solution.py:337
  114.7 0.2 fusion.2
  114.9 0.2 convolution_convert_fusion.1
  115.2 0.0 copy-start.2
  115.2 0.3 convolution_convert_fusion
  115.4 0.6 copy-done.2
  116.1 0.0 copy-start.4
  116.1 0.8 fusion
  116.9 0.0 copy-done.4
  (3 shorter events, 0.1 us)
Async XLA Ops:
  0.6 1.1 copy-start
  1.8 0.9 copy-start.1
  2.7 0.9 copy-start.3
  115.2 0.9 copy-start.2
  116.1 0.8 copy-start.4

commit v2 on v1

--- a/solution.py
+++ b/solution.py
@@ -327,25 +327,84 @@
         in_specs=[pl.BlockSpec(memory_space=pl.ANY)] * 3,
         out_specs=(pl.BlockSpec(memory_space=pltpu.VMEM), pl.BlockSpec(memory_space=pltpu.VMEM)),
         scratch_shapes=scratch,
-        compiler_params=pltpu.CompilerParams(collective_id=0, has_side_effects=True, vmem_limit_bytes=48 * 2**20),
+        compiler_params=pltpu.CompilerParams(collective_id=0, has_side_effects=True),
     )(old_basis, new_atoms, user_residuals)
 
 
-def finish_block(remainder_low, gram_matrix, coupling, user_residuals):
-    factor_lower = jnp.linalg.cholesky(gram_matrix)
-    identity = jnp.eye(gram_matrix.shape[0], dtype=F32)
-    inverse = jax.scipy.linalg.solve_triangular(factor_lower, identity, lower=True)
-    new_block = jnp.dot(remainder_low.astype(F32), inverse.T, precision=lax.Precision.HIGHEST).astype(BF16)
-    weights_low = jnp.dot(inverse, coupling, precision=lax.Precision.HIGHEST).astype(BF16)
-    updated = user_residuals.astype(F32) - jnp.dot(new_block, weights_low, preferred_element_type=F32)
-    return (new_block, updated.astype(BF16))
+def inverse_factor(work, n):
+    step = 8
+    for j in range(n // step):
+        top = j * step
+        block = work[top : top + step, :]
+        wide = block.shape
+        entry = {}
+        for k in range(step):
+            column = jnp.broadcast_to(block[:, top + k : top + k + 1], (step, n))
+            for i in range(k, step):
+                entry[i, k] = jnp.broadcast_to(column[i : i + 1, :], (step, n))
+        left = [jnp.broadcast_to(block[i : i + 1, :n], (step, n)) for i in range(step)]
+        right = [jnp.broadcast_to(block[i : i + 1, n:], (step, n)) for i in range(step)]
+        for i in range(step):
+            scale = lax.rsqrt(entry[i, i])
+            left[i] = left[i] * scale
+            right[i] = right[i] * scale
+            factor = {k: entry[k, i] * scale for k in range(i + 1, step)}
+            for k in range(i + 1, step):
+                for m in range(i + 1, k + 1):
+                    entry[k, m] = entry[k, m] - factor[k] * factor[m]
+                left[k] = left[k] - factor[k] * left[i]
+                right[k] = right[k] - factor[k] * right[i]
+        line = lax.broadcasted_iota(jnp.int32, (step, n), 0)
+        solved_left, solved_right = left[0], right[0]
+        for i in range(1, step):
+            solved_left = jnp.where(line == i, left[i], solved_left)
+            solved_right = jnp.where(line == i, right[i], solved_right)
+        work[top : top + step, n:] = solved_right
+        rest = top + step
+        if rest < n:
+            solved = jnp.concatenate([solved_left, solved_right], axis=1)
+            update = lax.dot_general(
+                solved_left[:, rest:], solved, (((0,), (0,)), ((), ())),
+                precision=lax.Precision.HIGHEST, preferred_element_type=F32,
+            )
+            work[rest:, :] = work[rest:, :] - update
+
+
+def finish_kernel(low, sums, users, block_out, updated_out, work):
+    n = low.shape[1]
+    lines = lax.broadcasted_iota(jnp.int32, (n, n), 0)
+    columns = lax.broadcasted_iota(jnp.int32, (n, n), 1)
+    work[:, :n] = sums[:, :n]
+    work[:, n:] = jnp.where(lines == columns, 1.0, 0.0)
+    inverse_factor(work, n)
+    inverse = work[:, n:]
+    weights = jnp.dot(inverse, sums[:, n:], precision=lax.Precision.HIGHEST, preferred_element_type=F32).astype(BF16)
+    new_block = lax.dot_general(
+        low[...].astype(F32), inverse, (((1,), (1,)), ((), ())),
+        precision=lax.Precision.HIGHEST, preferred_element_type=F32,
+    ).astype(BF16)
+    block_out[...] = new_block
+    updated = users[...].astype(F32) - jnp.dot(new_block, weights, preferred_element_type=F32)
+    updated_out[...] = updated.astype(BF16)
+
+
+def finish(remainder_low, sums, user_residuals):
+    rows, b = remainder_low.shape
+    u = user_residuals.shape[1]
+    return pl.pallas_call(
+        finish_kernel,
+        out_shape=(jax.ShapeDtypeStruct((rows, b), BF16), jax.ShapeDtypeStruct((rows, u), BF16)),
+        in_specs=[pl.BlockSpec(memory_space=pltpu.VMEM)] * 3,
+        out_specs=(pl.BlockSpec(memory_space=pltpu.VMEM), pl.BlockSpec(memory_space=pltpu.VMEM)),
+        scratch_shapes=[pltpu.VMEM((b, 2 * b), F32)],
+        compiler_params=pltpu.CompilerParams(vmem_limit_bytes=16 * 2**20),
+    )(remainder_low, sums, user_residuals)
 
 
 def local(old_basis, new_atoms, user_residuals):
     m_total = float(old_basis.shape[0] * lax.axis_size("rows"))
-    b = new_atoms.shape[1]
     remainder_low, sums = exchange(old_basis, new_atoms, user_residuals, m_total)
-    return finish_block(remainder_low, sums[:, :b], sums[:, b:], user_residuals)
+    return finish(remainder_low, sums, user_residuals)
 
 
 def solution(mesh):

time: 117 us -> 101 us (0.86)
  other arithmetic: 22.9 us -> 0 us
  Pallas kernels: 88 us -> 98.2 us
  local copies, waits for them, and re-layouts: 3.72 us -> 1.79 us
  matrix products: 1.52 us -> 0 us
    another operation x5 -> x0, other arithmetic: 22.9 us -> none  [the longest x3 12.4 us: finish_block(): factor_lower = jnp.linalg.cholesky(gram_matrix)]
    pallas_call x0 -> x1, Pallas kernels: none -> 9.53 us  [finish(): pl.pallas_call(finish_kernel, out_shape=(jax.ShapeDtypeStruct((rows, b),...]
    unnamed x10 -> x6, local copies, waits for them, and re-layouts: 3.54 us -> 1.79 us
    dot_general x3 -> x0, matrix products: 1.27 us -> none  [the longest x1 0.81 us: finish_block(): jnp.dot(new_block, weights_low, preferred_element_type=F32)]
where the time goes in v2:
time: 101 us
  Pallas kernels  98.2 us (97%)
  local copies, waits for them, and re-layouts  1.79 us (2%)
    pallas_call x1, Pallas kernels, exchange(): pl.pallas_call(functools.partial(exchange_kernel, m_total), out_shape=(ja...  88.7 us
    pallas_call x1, Pallas kernels, finish(): pl.pallas_call(finish_kernel, out_shape=(jax.ShapeDtypeStruct((rows, b),...  9.53 us

profile of v2, /device:TPU:1, one launch (start us, length us, event | category | flops | bytes accessed | tf_op | source)
XLA Modules:
  0.0 100.7 jit_solution(8550354960679236800)
XLA Ops:
  0.6 0.0 copy-start
  0.6 88.7 %shard_map.50 = (bf16[384,128]{1,0:T(8,128)(2,1)}, f32[128,256]{1,0:T(8,128)}) custom-call(bf16[384,1024]{1,0:T(8,128)(2,1)} %basis_hbm.1, bf16[384,128]{1,0:T(8,128)(2,1)} %atoms_hbm.1, bf16[384,128]{1,0:T(8,128)(2,1)} %users.1), custom_call_target="tpu_custom_call" | custom-call | tf_op jit(solution)/shard_map/pallas_call | solution.py:324
  89.3 0.0 copy-done
  89.3 0.0 copy-start.1
  89.3 0.9 copy-done.1
  90.2 0.0 copy-start.2
  90.2 0.9 copy-done.2
  91.1 9.5 %shard_map.51 = (bf16[384,128]{1,0:T(8,128)(2,1)}, bf16[384,128]{1,0:T(8,128)(2,1)}) custom-call(bf16[384,128]{1,0:T(8,128)(2,1)S(1)} %copy-done.2, f32[128,256]{1,0:T(8,128)S(1)} %copy-done.1, bf16[384,128]{1,0:T(8,128)(2,1)S(1)} %copy-done), custom_call_target="tpu_custom_call" | custom-call | tf_op jit(solution)/shard_map/pallas_call | solution.py:394
Async XLA Ops:
  0.6 88.7 %copy-start = (bf16[384,128]{1,0:T(8,128)(2,1)S(1)}, bf16[384,128]{1,0:T(8,128)(2,1)}, u32[]{:S(2)}) copy-start(bf16[384,128]{1,0:T(8,128)(2,1)} %users.1) | copy-start | bytes 294916
  89.3 0.9 copy-start.1
  90.2 0.9 copy-start.2

commit v3 on v2

--- a/solution.py
+++ b/solution.py
@@ -13,6 +13,7 @@
 Y, Z, CORES, X = 4, 16, 2, 4
 STRIPE = 2
 ROW_CHUNKS = 3
+GROUPS = 1
 
 
 def place():
@@ -50,10 +51,11 @@
     basis_hbm, atoms_hbm, users_hbm,
     low_out, sums_out,
     basis, atoms, users, low, remainder,
-    mate_out, mate_in, patch_out, patch_in, far_out, far_in, own_piece, coef, image, own_image,
+    mate_out, mate_in, patch_out, patch_in, far_out, far_in, own, coef, image, own_image, partial, meter, gmeter,
     gram_out, gram_in, gpatch_out, gpatch_in, gfar_in, gown, gpiece,
-    load_sem,
+    load_sem, left_sem, right_sem,
     mate_s, mate_r, patch_s, patch_r, far_s, far_r, gather_s, gather_r, users_s, users_r,
+    gmate_s, gmate_r, gpatch_s, gpatch_r, gfar_s, gfar_r, ggather_s, ggather_r,
 ):
     y, pair, stripe, core, x = place()
     pairs = Z // STRIPE
@@ -97,169 +99,222 @@
     barrier = pltpu.get_barrier_semaphore()
     peers = [mate]
     peers += [same_half(d) for d in patch_order] + [other_half(d) for d in patch_order]
-    peers += [far_device(d) for d in far_order] + [user_device(d) for d in user_order]
+    peers += [user_device(d) for d in user_order]
+    left_reach, right_reach = pairs // 2, (pairs - 1) // 2
+    if left_reach:
+        peers.append(far_device(1))
+    if right_reach:
+        peers.append(far_device(pairs - 1))
     for peer in peers:
         pl.semaphore_signal(barrier, inc=1, device_id=peer, device_id_type=MESH)
 
-    loads = [
-        pltpu.make_async_copy(atoms_hbm, atoms, load_sem.at[0]),
-        pltpu.make_async_copy(basis_hbm, basis, load_sem.at[1]),
-        pltpu.make_async_copy(users_hbm, users, load_sem.at[2]),
-    ]
+    width = piece_cols // GROUPS
+
+    def columns(g, stripe_index):
+        return pl.ds(stripe_index * piece_cols + g * width, width)
+
+    loads = [pltpu.make_async_copy(atoms_hbm, atoms, load_sem.at[0])]
+    for g in range(GROUPS):
+        for t in range(STRIPE):
+            cols = columns(g, t)
+            loads.append(pltpu.make_async_copy(basis_hbm.at[:, cols], basis.at[:, cols], load_sem.at[1 + g * STRIPE + t]))
+    loads.append(pltpu.make_async_copy(users_hbm, users, load_sem.at[1 + GROUPS * STRIPE]))
     for load in loads:
         load.start()
     loads[0].wait()
     low[...] = atoms[...]
     remainder[...] = atoms[...].astype(F32)
-    loads[1].wait()
-    loads[2].wait()
-    pl.semaphore_wait(barrier, len(peers))
+
+    def pass_on(distance):
+        if distance > 2:
+            if left_reach >= distance - 1:
+                pl.semaphore_wait(left_sem.at[distance - 3], 1)
+            if right_reach >= distance - 1:
+                pl.semaphore_wait(right_sem.at[distance - 3], 1)
+        if left_reach >= distance:
+            pl.semaphore_signal(left_sem.at[distance - 2], inc=1, device_id=far_device(1), device_id_type=MESH)
+        if right_reach >= distance:
+            pl.semaphore_signal(right_sem.at[distance - 2], inc=1, device_id=far_device(pairs - 1), device_id_type=MESH)
 
     def remote(src, dst, send, recv, peer):
         return pltpu.make_async_remote_copy(
             src_ref=src, dst_ref=dst, send_sem=send, recv_sem=recv, device_id=peer, device_id_type=MESH
         )
 
+    def settle(like, count, sem):
+        if count:
+            pltpu.make_async_copy(like.at[pl.ds(0, count)], like.at[pl.ds(0, count)], sem).wait()
+
+    piece_at = pl.ds(pl.multiple_of(y * piece_rows, piece_rows), piece_rows)
+    keep_at = pl.ds(pl.multiple_of(half * side, side), side)
+    give_at = pl.ds(pl.multiple_of((1 - half) * side, side), side)
+    own_width = pl.ds(pl.multiple_of(stripe * width, width), width)
+
     for sweep in range(2):
-        sent = []
         turned = low[...].astype(F32).T.astype(BF16)
-        halves = []
         mates = []
-        for s in range(STRIPE):
-            cols = pl.ds(s * piece_cols, piece_cols)
-            product = jnp.dot(turned, basis[:, cols], preferred_element_type=F32)
-            own_piece[:, cols] = product
-            mate_out[sweep, :, cols] = own_piece[pl.ds(pl.multiple_of((1 - half) * side, side), side), cols].astype(BF16)
-            copy = remote(
-                mate_out.at[sweep, :, cols], mate_in.at[sweep, :, cols],
-                mate_s.at[sweep, s], mate_r.at[sweep, s], mate,
-            )
+        for g in range(GROUPS):
+            for t in range(STRIPE):
+                if sweep == 0:
+                    loads[1 + g * STRIPE + t].wait()
+                own[g, :, t * width : (t + 1) * width] = jnp.dot(
+                    turned, basis[:, columns(g, t)], preferred_element_type=F32
+                )
+            mate_out[sweep, g] = own[g, give_at, :].astype(BF16)
+            if sweep == 0 and g == 0:
+                pl.semaphore_wait(barrier, len(peers))
+                pass_on(2)
+            copy = remote(mate_out.at[sweep, g], mate_in.at[sweep, g], mate_s.at[sweep, g], mate_r.at[sweep, g], mate)
             copy.start()
             mates.append(copy)
-        sent += mates
-        for s in range(STRIPE):
-            cols = pl.ds(s * piece_cols, piece_cols)
-            mates[s].wait_recv()
-            total = own_piece[pl.ds(pl.multiple_of(half * side, side), side), cols] + mate_in[sweep, :, cols].astype(F32)
-            patch_out[sweep, :, cols] = total.astype(BF16)
         patch_copies = []
-        for i, d in enumerate(patch_order):
-            other, other_y, other_stripe = patch_device(d)
-            src = patch_out.at[
+        for g in range(GROUPS):
+            mates[g].wait_recv()
+            patch_out[sweep, g] = (own[g, keep_at, :] + mate_in[sweep, g].astype(F32)).astype(BF16)
+            copies = []
+            for i, d in enumerate(patch_order):
+                other, other_y, other_stripe = patch_device(d)
+                src = patch_out.at[
+                    sweep, g,
+                    pl.ds(pl.multiple_of(other_y * piece_rows, piece_rows), piece_rows),
+                    pl.ds(pl.multiple_of(other_stripe * width, width), width),
+                ]
+                copy = remote(
+                    src, patch_in.at[sweep, g, owner], patch_s.at[sweep, g], patch_r.at[sweep, g], same_half(d)
+                )
+                copy.start()
+                copies.append(copy)
+            patch_in[sweep, g, owner] = patch_out[sweep, g, piece_at, own_width]
+            patch_copies.append(copies)
+        if sweep == 0:
+            pass_on(3)
+        far_copies = []
+        for g in range(GROUPS):
+            if sweep == 0 and g == 0:
+                pass_on(4)
+            settle(meter, len(patch_order), patch_r.at[sweep, g])
+            total = patch_in[sweep, g, 0].astype(F32)
+            for j in range(1, owners):
+                total = total + patch_in[sweep, g, j].astype(F32)
+            far_out[sweep, g] = total.astype(BF16)
+            if sweep == 0 and g == 0:
+                pass_on(5)
+            copies = []
+            for i, d in enumerate(far_order):
+                copy = remote(
+                    far_out.at[sweep, g], far_in.at[sweep, g, pair], far_s.at[sweep, g], far_r.at[sweep, g],
+                    far_device(d),
+                )
+                copy.start()
+                copies.append(copy)
+            far_in[sweep, g, pair] = far_out[sweep, g]
+            far_copies.append(copies)
+        gathers = []
+        for g in range(GROUPS):
+            settle(meter, len(far_order), far_r.at[sweep, g])
+            total = far_in[sweep, g, 0].astype(F32)
+            for j in range(1, pairs):
+                total = total + far_in[sweep, g, j].astype(F32)
+            mine = coef.at[
                 sweep,
-                pl.ds(pl.multiple_of(other_y * piece_rows, piece_rows), piece_rows),
-                pl.ds(pl.multiple_of(other_stripe * piece_cols, piece_cols), piece_cols),
+                pl.ds(pl.multiple_of(half * side + y * piece_rows, piece_rows), piece_rows),
+                pl.ds(pl.multiple_of(stripe * piece_cols + g * width, width), width),
             ]
-            copy = remote(src, patch_in.at[sweep, owner], patch_s.at[sweep, i], patch_r.at[sweep, i], same_half(d))
-            copy.start()
-            patch_copies.append(copy)
-        patch_in[sweep, owner] = patch_out[
-            sweep,
-            pl.ds(pl.multiple_of(y * piece_rows, piece_rows), piece_rows),
-            pl.ds(pl.multiple_of(stripe * piece_cols, piece_cols), piece_cols),
-        ]
-        for copy in patch_copies:
-            copy.wait_recv()
-        sent += patch_copies
-        total = patch_in[sweep, 0].astype(F32)
-        for j in range(1, owners):
-            total = total + patch_in[sweep, j].astype(F32)
-        far_out[sweep] = total.astype(BF16)
-        far_copies = []
-        for i, d in enumerate(far_order):
-            copy = remote(far_out.at[sweep], far_in.at[sweep, pair], far_s.at[sweep, i], far_r.at[sweep, i], far_device(d))
-            copy.start()
-            far_copies.append(copy)
-        far_in[sweep, pair] = far_out[sweep]
-        for copy in far_copies:
-            copy.wait_recv()
-        sent += far_copies
-        total = far_in[sweep, 0].astype(F32)
-        for j in range(1, pairs):
-            total = total + far_in[sweep, j].astype(F32)
-        mine = coef.at[
-            sweep,
-            pl.ds(pl.multiple_of(half * side + y * piece_rows, piece_rows), piece_rows),
-            pl.ds(pl.multiple_of(stripe * piece_cols, piece_cols), piece_cols),
-        ]
-        mine[...] = (total / m_total).astype(BF16)
-        gathers = []
-        for i, d in enumerate(patch_order):
-            for j, target in enumerate((same_half(d), other_half(d))):
-                copy = remote(mine, mine, gather_s.at[sweep, 2 * i + j], gather_r.at[sweep, 2 * i + j], target)
+            mine[...] = (total / m_total).astype(BF16)
+            targets = [mate]
+            for d in patch_order:
+                targets += [same_half(d), other_half(d)]
+            targets = targets[1:] + targets[:1]
+            copies = []
+            for i, target in enumerate(targets):
+                copy = remote(mine, mine, gather_s.at[sweep, g], gather_r.at[sweep, g], target)
                 copy.start()
-                gathers.append(copy)
-        copy = remote(mine, mine, gather_s.at[sweep, 2 * owners - 2], gather_r.at[sweep, 2 * owners - 2], mate)
-        copy.start()
-        gathers.append(copy)
-        for copy in gathers:
-            copy.wait_recv()
-        sent += gathers
-
+                copies.append(copy)
+            gathers.append(copies)
+
+        def image_part(rows_at, g):
+            out = None
+            for t in range(STRIPE):
+                cols = columns(g, t)
+                term = lax.dot_general(
+                    basis[rows_at, cols], coef[sweep, :, cols], (((1,), (1,)), ((), ())), preferred_element_type=F32
+                )
+                out = term if out is None else out + term
+            return out
+
+        for g in range(GROUPS):
+            settle(meter, len(gathers[g]), gather_r.at[sweep, g])
+            if g < GROUPS - 1:
+                for c in range(ROW_CHUNKS):
+                    part = pl.ds(c * chunk, chunk)
+                    term = image_part(part, g)
+                    partial[part, :] = term if g == 0 else partial[part, :] + term
         user_copies = []
         for c in range(ROW_CHUNKS):
             part = pl.ds(c * chunk, chunk)
-            product = lax.dot_general(
-                basis[part, :], coef[sweep], (((1,), (1,)), ((), ())), preferred_element_type=F32
-            )
+            product = image_part(part, GROUPS - 1)
+            if GROUPS > 1:
+                product = product + partial[part, :]
             own_image[sweep, part, :] = product.astype(BF16)
             for i, d in enumerate(user_order):
                 copy = remote(
                     own_image.at[sweep, part, :], image.at[sweep, x, part, :],
-                    users_s.at[sweep, c, i], users_r.at[sweep, c, i], user_device(d),
+                    users_s.at[sweep], users_r.at[sweep, c], user_device(d),
                 )
                 copy.start()
                 user_copies.append(copy)
             image[sweep, x, part, :] = own_image[sweep, part, :]
         for c in range(ROW_CHUNKS):
             part = pl.ds(c * chunk, chunk)
-            for copy in user_copies[c * len(user_order) : (c + 1) * len(user_order)]:
-                copy.wait_recv()
+            if user_order:
+                arrived = image.at[sweep, pl.ds(0, len(user_order)), part, :]
+                pltpu.make_async_copy(arrived, arrived, users_r.at[sweep, c]).wait()
             projected = image[sweep, 0, part, :].astype(F32)
             for j in range(1, X):
                 projected = projected + image[sweep, j, part, :].astype(F32)
             left = remainder[part, :] - projected
             remainder[part, :] = left
             low[part, :] = left.astype(BF16)
-        sent += user_copies
-        for copy in sent:
-            copy.wait_send()
+        for g in range(GROUPS):
+            mates[g].wait_send()
+            settle(meter, len(patch_order), patch_s.at[sweep, g])
+            settle(meter, len(far_order), far_s.at[sweep, g])
+            settle(meter, len(gathers[g]), gather_s.at[sweep, g])
+        if user_order:
+            gone = image.at[sweep, pl.ds(0, len(user_order)), :, :]
+            pltpu.make_async_copy(gone, gone, users_s.at[sweep]).wait()
 
     low_out[...] = low[...]
+    loads[-1].wait()
     turned = low[...].astype(F32).T.astype(BF16)
     gown[:, :atoms_b] = jnp.dot(turned, low[...], preferred_element_type=F32)
     gown[:, atoms_b:] = jnp.dot(turned, users[...], preferred_element_type=F32)
     gram_out[...] = gown[pl.ds(pl.multiple_of((1 - half) * side, side), side), :]
-    sent = []
-    copy = remote(gram_out, gram_in, mate_s.at[2, 0], mate_r.at[2, 0], mate)
+    copy = remote(gram_out, gram_in, gmate_s.at[0], gmate_r.at[0], mate)
     copy.start()
-    sent.append(copy)
+    mate_copy = copy
     copy.wait_recv()
     gpatch_out[...] = gown[pl.ds(pl.multiple_of(half * side, side), side), :] + gram_in[...]
     patch_copies = []
     for i, d in enumerate(patch_order):
         other, _, _ = patch_device(d)
         src = gpatch_out.at[pl.ds(pl.multiple_of(other * gram_rows, gram_rows), gram_rows), :]
-        copy = remote(src, gpatch_in.at[owner], patch_s.at[2, i], patch_r.at[2, i], same_half(d))
+        copy = remote(src, gpatch_in.at[owner], gpatch_s.at[0], gpatch_r.at[0], same_half(d))
         copy.start()
         patch_copies.append(copy)
     gpatch_in[owner] = gpatch_out[pl.ds(pl.multiple_of(owner * gram_rows, gram_rows), gram_rows), :]
-    for copy in patch_copies:
-        copy.wait_recv()
-    sent += patch_copies
+    settle(gmeter, len(patch_copies), gpatch_r.at[0])
     total = gpatch_in[0]
     for j in range(1, owners):
         total = total + gpatch_in[j]
     gpiece[...] = total
     far_copies = []
     for i, d in enumerate(far_order):
-        copy = remote(gpiece, gfar_in.at[pair], far_s.at[2, i], far_r.at[2, i], far_device(d))
+        copy = remote(gpiece, gfar_in.at[pair], gfar_s.at[0], gfar_r.at[0], far_device(d))
         copy.start()
         far_copies.append(copy)
     gfar_in[pair] = gpiece[...]
-    for copy in far_copies:
-        copy.wait_recv()
-    sent += far_copies
+    settle(gmeter, len(far_copies), gfar_r.at[0])
     total = gfar_in[0]
     for j in range(1, pairs):
         total = total + gfar_in[j]
@@ -268,17 +323,17 @@
     gathers = []
     for i, d in enumerate(patch_order):
         for j, target in enumerate((same_half(d), other_half(d))):
-            copy = remote(mine, mine, gather_s.at[2, 2 * i + j], gather_r.at[2, 2 * i + j], target)
+            copy = remote(mine, mine, ggather_s.at[0], ggather_r.at[0], target)
             copy.start()
             gathers.append(copy)
-    copy = remote(mine, mine, gather_s.at[2, 2 * owners - 2], gather_r.at[2, 2 * owners - 2], mate)
+    copy = remote(mine, mine, ggather_s.at[0], ggather_r.at[0], mate)
     copy.start()
     gathers.append(copy)
-    for copy in gathers:
-        copy.wait_recv()
-    sent += gathers
-    for copy in sent:
-        copy.wait_send()
+    settle(gmeter, len(gathers), ggather_r.at[0])
+    mate_copy.wait_send()
+    settle(gmeter, len(patch_copies), gpatch_s.at[0])
+    settle(gmeter, len(far_copies), gfar_s.at[0])
+    settle(gmeter, len(gathers), ggather_s.at[0])
 
 
 def exchange(old_basis, new_atoms, user_residuals, m_total):
@@ -287,26 +342,29 @@
     u = user_residuals.shape[1]
     owners, pairs = Y * STRIPE, Z // STRIPE
     side = b // 2
-    piece = (side // Y, k_loc // STRIPE)
+    width = k_loc // STRIPE // GROUPS
+    piece = (side // Y, width)
     gram_piece = (side // owners, b + u)
-    dma = pltpu.SemaphoreType.DMA
-    n_gather = 2 * owners - 1
+    dma, signal = pltpu.SemaphoreType.DMA, pltpu.SemaphoreType.REGULAR
     scratch = [
         pltpu.VMEM((rows, k_loc), BF16),
         pltpu.VMEM((rows, b), BF16),
         pltpu.VMEM((rows, u), BF16),
         pltpu.VMEM((rows, b), BF16),
         pltpu.VMEM((rows, b), F32),
-        pltpu.VMEM((2, side, k_loc), BF16),
-        pltpu.VMEM((2, side, k_loc), BF16),
-        pltpu.VMEM((2, side, k_loc), BF16),
-        pltpu.VMEM((2, owners, *piece), BF16),
-        pltpu.VMEM((2, *piece), BF16),
-        pltpu.VMEM((2, pairs, *piece), BF16),
-        pltpu.VMEM((b, k_loc), F32),
+        pltpu.VMEM((2, GROUPS, side, STRIPE * width), BF16),
+        pltpu.VMEM((2, GROUPS, side, STRIPE * width), BF16),
+        pltpu.VMEM((2, GROUPS, side, STRIPE * width), BF16),
+        pltpu.VMEM((2, GROUPS, owners, *piece), BF16),
+        pltpu.VMEM((2, GROUPS, *piece), BF16),
+        pltpu.VMEM((2, GROUPS, pairs, *piece), BF16),
+        pltpu.VMEM((GROUPS, b, STRIPE * width), F32),
         pltpu.VMEM((2, b, k_loc), BF16),
         pltpu.VMEM((2, X, rows, b), BF16),
         pltpu.VMEM((2, rows, b), BF16),
+        pltpu.VMEM((rows, b), F32),
+        pltpu.VMEM((2 * owners, *piece), BF16),
+        pltpu.VMEM((2 * owners, *gram_piece), F32),
         pltpu.VMEM((side, b + u), F32),
         pltpu.VMEM((side, b + u), F32),
         pltpu.VMEM((side, b + u), F32),
@@ -314,12 +372,10 @@
         pltpu.VMEM((pairs, *gram_piece), F32),
         pltpu.VMEM((b, b + u), F32),
         pltpu.VMEM(gram_piece, F32),
-        dma((3,)),
-        dma((3, STRIPE)), dma((3, STRIPE)),
-        dma((3, max(owners - 1, 1))), dma((3, max(owners - 1, 1))),
-        dma((3, max(pairs - 1, 1))), dma((3, max(pairs - 1, 1))),
-        dma((3, n_gather)), dma((3, n_gather)),
-        dma((2, ROW_CHUNKS, max(X - 1, 1))), dma((2, ROW_CHUNKS, max(X - 1, 1))),
+        dma((2 + GROUPS * STRIPE,)), signal((3,)), signal((2,)),
+        *[dma((2, GROUPS))] * 8,
+        dma((2,)), dma((2, ROW_CHUNKS)),
+        *[dma((1,))] * 8,
     ]
     return pl.pallas_call(
         functools.partial(exchange_kernel, m_total),

time: 101 us -> 96.8 us (0.958)
  Pallas kernels: 98.2 us -> 94.2 us
    pallas_call x1, Pallas kernels: 88.7 us -> 84.7 us  [exchange(): pl.pallas_call(functools.partial(exchange_kernel, m_total), out_shape=(ja...]
where the time goes in v3:
time: 96.8 us; the launch traced here: 96.7 us
  Pallas kernels  94.2 us (97%)
  local copies, waits for them, and re-layouts  1.79 us (2%)
    pallas_call x1, Pallas kernels, exchange(): pl.pallas_call(functools.partial(exchange_kernel, m_total), out_shape=(ja...  84.7 us
    pallas_call x1, Pallas kernels, finish(): pl.pallas_call(finish_kernel, out_shape=(jax.ShapeDtypeStruct((rows, b),...  9.53 us

profile of v3, /device:TPU:1, one launch (start us, length us, event | category | flops | bytes accessed | tf_op | source)
XLA Modules:
  0.0 96.7 jit_solution(2440357287796566264)
XLA Ops:
  0.6 0.0 copy-start
  0.6 84.7 %shard_map.50 = (bf16[384,128]{1,0:T(8,128)(2,1)}, f32[128,256]{1,0:T(8,128)}) custom-call(bf16[384,1024]{1,0:T(8,128)(2,1)} %basis_hbm.1, bf16[384,128]{1,0:T(8,128)(2,1)} %atoms_hbm.1, bf16[384,128]{1,0:T(8,128)(2,1)} %users.1), custom_call_target="tpu_custom_call" | custom-call | tf_op jit(solution)/shard_map/pallas_call | solution.py:380
  85.3 0.0 copy-done
  85.3 0.0 copy-start.1
  85.3 0.9 copy-done.1
  86.2 0.0 copy-start.2
  86.2 0.9 copy-done.2
  87.1 9.5 %shard_map.51 = (bf16[384,128]{1,0:T(8,128)(2,1)}, bf16[384,128]{1,0:T(8,128)(2,1)}) custom-call(bf16[384,128]{1,0:T(8,128)(2,1)S(1)} %copy-done.2, f32[128,256]{1,0:T(8,128)S(1)} %copy-done.1, bf16[384,128]{1,0:T(8,128)(2,1)S(1)} %copy-done), custom_call_target="tpu_custom_call" | custom-call | tf_op jit(solution)/shard_map/pallas_call | solution.py:450
Async XLA Ops:
  0.6 84.7 %copy-start = (bf16[384,128]{1,0:T(8,128)(2,1)S(1)}, bf16[384,128]{1,0:T(8,128)(2,1)}, u32[]{:S(2)}) copy-start(bf16[384,128]{1,0:T(8,128)(2,1)} %users.1) | copy-start | bytes 294916
  85.3 0.9 copy-start.1
  86.2 0.9 copy-start.2

commit v4 on v3

--- a/solution.py
+++ b/solution.py
@@ -14,6 +14,7 @@
 STRIPE = 2
 ROW_CHUNKS = 3
 GROUPS = 1
+STEP, SUB = 16, 8
 
 
 def place():
@@ -46,12 +47,54 @@
     return sorted(range(1, n), key=lambda d: -min(d, n - d))
 
 
+def inverse_factor(work, spread, n):
+    step = STEP
+    lane = lax.broadcasted_iota(jnp.int32, (step, n), 1)
+    line = lax.broadcasted_iota(jnp.int32, (step, n), 0)
+    for j in range(n // step):
+        top = j * step
+        rest = top + step
+        block = work[top:rest, :]
+        for k in range(step):
+            spread[step * k : step * (k + 1), :] = jnp.broadcast_to(block[:, top + k : top + k + 1], (step, n))
+        entry = {(i, k): spread[pl.ds(step * k + i, SUB, stride=0), :] for k in range(step) for i in range(k, step)}
+        inside = (lane[:SUB] >= top) & (lane[:SUB] < rest)
+        row = [
+            jnp.where(inside, jnp.where(lane[:SUB] == top + i, 1.0, 0.0), work[pl.ds(top + i, SUB, stride=0), :])
+            for i in range(step)
+        ]
+        for i in range(step):
+            scale = lax.rsqrt(entry[i, i])
+            row[i] = row[i] * scale
+            factor = {k: entry[k, i] * scale for k in range(i + 1, step)}
+            for k in range(i + 1, step):
+                for m in range(i + 1, k + 1):
+                    entry[k, m] = entry[k, m] - factor[k] * factor[m]
+                row[k] = row[k] - factor[k] * row[i]
+        parts = []
+        for h in range(step // SUB):
+            part = row[h * SUB]
+            for i in range(1, SUB):
+                part = jnp.where(line[:SUB] == i, row[h * SUB + i], part)
+            parts.append(part)
+        solved = parts[0] if len(parts) == 1 else jnp.concatenate(parts, axis=0)
+        work[top:rest, :] = solved
+        if rest < n:
+            update = lax.dot_general(
+                solved[:, rest:], solved, (((0,), (0,)), ((), ())),
+                precision=lax.Precision.HIGHEST, preferred_element_type=F32,
+            )
+            wide = lax.broadcasted_iota(jnp.int32, (n - rest, n), 1)
+            below = jnp.where((wide >= top) & (wide < rest), 0.0, work[rest:, :])
+            work[rest:, :] = below - update
+
+
 def exchange_kernel(
     m_total,
     basis_hbm, atoms_hbm, users_hbm,
-    low_out, sums_out,
+    block_out, updated_out,
     basis, atoms, users, low, remainder,
-    mate_out, mate_in, patch_out, patch_in, far_out, far_in, own, coef, image, own_image, partial, meter, gmeter,
+    mate_out, mate_in, patch_out, patch_in, far_out, far_in, own, coef, image, own_image, partial, meter, gmeter, sums, factor, spread,
     gram_out, gram_in, gpatch_out, gpatch_in, gfar_in, gown, gpiece,
     load_sem, left_sem, right_sem,
     mate_s, mate_r, patch_s, patch_r, far_s, far_r, gather_s, gather_r, users_s, users_r,
@@ -284,7 +327,6 @@
             gone = image.at[sweep, pl.ds(0, len(user_order)), :, :]
             pltpu.make_async_copy(gone, gone, users_s.at[sweep]).wait()
 
-    low_out[...] = low[...]
     loads[-1].wait()
     turned = low[...].astype(F32).T.astype(BF16)
     gown[:, :atoms_b] = jnp.dot(turned, low[...], preferred_element_type=F32)
@@ -318,7 +360,7 @@
     total = gfar_in[0]
     for j in range(1, pairs):
         total = total + gfar_in[j]
-    mine = sums_out.at[pl.ds(pl.multiple_of(half * side + owner * gram_rows, gram_rows), gram_rows), :]
+    mine = sums.at[pl.ds(pl.multiple_of(half * side + owner * gram_rows, gram_rows), gram_rows), :]
     mine[...] = total / m_total
     gathers = []
     for i, d in enumerate(patch_order):
@@ -330,6 +372,21 @@
     copy.start()
     gathers.append(copy)
     settle(gmeter, len(gathers), ggather_r.at[0])
+    factor[...] = sums[:, :atoms_b]
+    inverse_factor(factor, spread, atoms_b)
+    lines = lax.broadcasted_iota(jnp.int32, (atoms_b, atoms_b), 0)
+    lanes = lax.broadcasted_iota(jnp.int32, (atoms_b, atoms_b), 1)
+    inverse = jnp.where(lines >= lanes, factor[...], 0.0)
+    weights = jnp.dot(
+        inverse, sums[:, atoms_b:], precision=lax.Precision.HIGHEST, preferred_element_type=F32
+    ).astype(BF16)
+    new_block = lax.dot_general(
+        low[...].astype(F32), inverse, (((1,), (1,)), ((), ())),
+        precision=lax.Precision.HIGHEST, preferred_element_type=F32,
+    ).astype(BF16)
+    block_out[...] = new_block
+    updated = users[...].astype(F32) - jnp.dot(new_block, weights, preferred_element_type=F32)
+    updated_out[...] = updated.astype(BF16)
     mate_copy.wait_send()
     settle(gmeter, len(patch_copies), gpatch_s.at[0])
     settle(gmeter, len(far_copies), gfar_s.at[0])
@@ -365,6 +422,9 @@
         pltpu.VMEM((rows, b), F32),
         pltpu.VMEM((2 * owners, *piece), BF16),
         pltpu.VMEM((2 * owners, *gram_piece), F32),
+        pltpu.VMEM((b, b + u), F32),
+        pltpu.VMEM((b, b), F32),
+        pltpu.VMEM((STEP * STEP, b), F32),
         pltpu.VMEM((side, b + u), F32),
         pltpu.VMEM((side, b + u), F32),
         pltpu.VMEM((side, b + u), F32),
@@ -379,88 +439,17 @@
     ]
     return pl.pallas_call(
         functools.partial(exchange_kernel, m_total),
-        out_shape=(jax.ShapeDtypeStruct((rows, b), BF16), jax.ShapeDtypeStruct((b, b + u), F32)),
+        out_shape=(jax.ShapeDtypeStruct((rows, b), BF16), jax.ShapeDtypeStruct((rows, u), BF16)),
         in_specs=[pl.BlockSpec(memory_space=pl.ANY)] * 3,
         out_specs=(pl.BlockSpec(memory_space=pltpu.VMEM), pl.BlockSpec(memory_space=pltpu.VMEM)),
         scratch_shapes=scratch,
-        compiler_params=pltpu.CompilerParams(collective_id=0, has_side_effects=True),
+        compiler_params=pltpu.CompilerParams(collective_id=0, has_side_effects=True, vmem_limit_bytes=55000 * 1024),
     )(old_basis, new_atoms, user_residuals)
-
-
-def inverse_factor(work, n):
-    step = 8
-    for j in range(n // step):
-        top = j * step
-        block = work[top : top + step, :]
-        wide = block.shape
-        entry = {}
-        for k in range(step):
-            column = jnp.broadcast_to(block[:, top + k : top + k + 1], (step, n))
-            for i in range(k, step):
-                entry[i, k] = jnp.broadcast_to(column[i : i + 1, :], (step, n))
-        left = [jnp.broadcast_to(block[i : i + 1, :n], (step, n)) for i in range(step)]
-        right = [jnp.broadcast_to(block[i : i + 1, n:], (step, n)) for i in range(step)]
-        for i in range(step):
-            scale = lax.rsqrt(entry[i, i])
-            left[i] = left[i] * scale
-            right[i] = right[i] * scale
-            factor = {k: entry[k, i] * scale for k in range(i + 1, step)}
-            for k in range(i + 1, step):
-                for m in range(i + 1, k + 1):
-                    entry[k, m] = entry[k, m] - factor[k] * factor[m]
-                left[k] = left[k] - factor[k] * left[i]
-                right[k] = right[k] - factor[k] * right[i]
-        line = lax.broadcasted_iota(jnp.int32, (step, n), 0)
-        solved_left, solved_right = left[0], right[0]
-        for i in range(1, step):
-            solved_left = jnp.where(line == i, left[i], solved_left)
-            solved_right = jnp.where(line == i, right[i], solved_right)
-        work[top : top + step, n:] = solved_right
-        rest = top + step
-        if rest < n:
-            solved = jnp.concatenate([solved_left, solved_right], axis=1)
-            update = lax.dot_general(
-                solved_left[:, rest:], solved, (((0,), (0,)), ((), ())),
-                precision=lax.Precision.HIGHEST, preferred_element_type=F32,
-            )
-            work[rest:, :] = work[rest:, :] - update
-
-
-def finish_kernel(low, sums, users, block_out, updated_out, work):
-    n = low.shape[1]
-    lines = lax.broadcasted_iota(jnp.int32, (n, n), 0)
-    columns = lax.broadcasted_iota(jnp.int32, (n, n), 1)
-    work[:, :n] = sums[:, :n]
-    work[:, n:] = jnp.where(lines == columns, 1.0, 0.0)
-    inverse_factor(work, n)
-    inverse = work[:, n:]
-    weights = jnp.dot(inverse, sums[:, n:], precision=lax.Precision.HIGHEST, preferred_element_type=F32).astype(BF16)
-    new_block = lax.dot_general(
-        low[...].astype(F32), inverse, (((1,), (1,)), ((), ())),
-        precision=lax.Precision.HIGHEST, preferred_element_type=F32,
-    ).astype(BF16)
-    block_out[...] = new_block
-    updated = users[...].astype(F32) - jnp.dot(new_block, weights, preferred_element_type=F32)
-    updated_out[...] = updated.astype(BF16)
-
-
-def finish(remainder_low, sums, user_residuals):
-    rows, b = remainder_low.shape
-    u = user_residuals.shape[1]
-    return pl.pallas_call(
-        finish_kernel,
-        out_shape=(jax.ShapeDtypeStruct((rows, b), BF16), jax.ShapeDtypeStruct((rows, u), BF16)),
-        in_specs=[pl.BlockSpec(memory_space=pltpu.VMEM)] * 3,
-        out_specs=(pl.BlockSpec(memory_space=pltpu.VMEM), pl.BlockSpec(memory_space=pltpu.VMEM)),
-        scratch_shapes=[pltpu.VMEM((b, 2 * b), F32)],
-        compiler_params=pltpu.CompilerParams(vmem_limit_bytes=16 * 2**20),
-    )(remainder_low, sums, user_residuals)
 
 
 def local(old_basis, new_atoms, user_residuals):
     m_total = float(old_basis.shape[0] * lax.axis_size("rows"))
-    remainder_low, sums = exchange(old_basis, new_atoms, user_residuals, m_total)
-    return finish(remainder_low, sums, user_residuals)
+    return exchange(old_basis, new_atoms, user_residuals, m_total)
 
 
 def solution(mesh):

time: 96.8 us -> 91.8 us (0.948)
  Pallas kernels: 94.2 us -> 89.8 us
    pallas_call x1 -> x0, Pallas kernels: 9.53 us -> none  [finish(): pl.pallas_call(finish_kernel, out_shape=(jax.ShapeDtypeStruct((rows, b),...]
    pallas_call x1, Pallas kernels: 84.7 us -> 89.8 us  [exchange(): pl.pallas_call(functools.partial(exchange_kernel, m_total), out_shape=(ja...]
where the time goes in v4:
time: 91.8 us; the launch traced here: 91.7 us
  Pallas kernels  89.8 us (98%)
  local copies, waits for them, and re-layouts  1.28 us (1%)
    pallas_call x1, Pallas kernels, exchange(): pl.pallas_call(functools.partial(exchange_kernel, m_total), out_shape=(ja...  89.8 us

profile of v4, /device:TPU:1, one launch (start us, length us, event | category | flops | bytes accessed | tf_op | source)
XLA Modules:
  0.0 91.7 jit_solution(8948551450335852246)
XLA Ops:
  0.6 89.8 %shard_map.50 = (bf16[384,128]{1,0:T(8,128)(2,1)S(1)}, bf16[384,128]{1,0:T(8,128)(2,1)S(1)}) custom-call(bf16[384,1024]{1,0:T(8,128)(2,1)} %basis_hbm.1, bf16[384,128]{1,0:T(8,128)(2,1)} %atoms_hbm.1, bf16[384,128]{1,0:T(8,128)(2,1)} %users_hbm.1), custom_call_target="tpu_custom_call" | custom-call | tf_op jit(solution)/shard_map/pallas_call | solution.py:440
  90.4 0.6 copy.7
  91.1 0.6 copy.8

commit v5 on v4

--- a/solution.py
+++ b/solution.py
@@ -13,7 +13,7 @@
 Y, Z, CORES, X = 4, 16, 2, 4
 STRIPE = 2
 ROW_CHUNKS = 3
-GROUPS = 1
+GROUPS = 2
 STEP, SUB = 16, 8
 
 
@@ -92,13 +92,13 @@
 def exchange_kernel(
     m_total,
     basis_hbm, atoms_hbm, users_hbm,
-    block_out, updated_out,
+    both_out,
     basis, atoms, users, low, remainder,
-    mate_out, mate_in, patch_out, patch_in, far_out, far_in, own, coef, image, own_image, partial, meter, gmeter, sums, factor, spread,
-    gram_out, gram_in, gpatch_out, gpatch_in, gfar_in, gown, gpiece,
+    patch_out, patch_in, far_out, far_in, coef, image, own_image, partial, meter, gmeter, sums, factor, spread,
+    gpatch_in, gfar_in, gown, gpiece,
     load_sem, left_sem, right_sem,
-    mate_s, mate_r, patch_s, patch_r, far_s, far_r, gather_s, gather_r, users_s, users_r,
-    gmate_s, gmate_r, gpatch_s, gpatch_r, gfar_s, gfar_r, ggather_s, ggather_r,
+    patch_s, patch_r, far_s, far_r, gather_s, gather_r, users_s, users_r,
+    gpatch_s, gpatch_r, gfar_s, gfar_r, ggather_s, ggather_r,
 ):
     y, pair, stripe, core, x = place()
     pairs = Z // STRIPE
@@ -134,14 +134,19 @@
     def user_device(shift):
         return device(y, pair, stripe, core, lax.rem(x + shift, X))
 
-    mate = device(y, pair, stripe, 1 - core, x)
     patch_order = sorted(range(1, owners), key=lambda d: -min(d, owners - d))
     far_order = ring_order(pairs)
     user_order = ring_order(X)
+    spots = owners * 2
+    spot = owner * 2 + half
+    patch = []
+    for d in patch_order:
+        other, other_y, other_stripe = patch_device(d)
+        patch += [(half, other, other_y, other_stripe, same_half(d)), (1 - half, other, other_y, other_stripe, other_half(d))]
+    patch.append((1 - half, owner, y, stripe, device(y, pair, stripe, 1 - core, x)))
 
     barrier = pltpu.get_barrier_semaphore()
-    peers = [mate]
-    peers += [same_half(d) for d in patch_order] + [other_half(d) for d in patch_order]
+    peers = [target for *_, target in patch]
     peers += [user_device(d) for d in user_order]
     left_reach, right_reach = pairs // 2, (pairs - 1) // 2
     if left_reach:
@@ -188,56 +193,40 @@
         if count:
             pltpu.make_async_copy(like.at[pl.ds(0, count)], like.at[pl.ds(0, count)], sem).wait()
 
-    piece_at = pl.ds(pl.multiple_of(y * piece_rows, piece_rows), piece_rows)
-    keep_at = pl.ds(pl.multiple_of(half * side, side), side)
-    give_at = pl.ds(pl.multiple_of((1 - half) * side, side), side)
     own_width = pl.ds(pl.multiple_of(stripe * width, width), width)
+
+    def piece_at(h, at_y):
+        return pl.ds(pl.multiple_of(h * side + at_y * piece_rows, piece_rows), piece_rows)
 
     for sweep in range(2):
         turned = low[...].astype(F32).T.astype(BF16)
-        mates = []
         for g in range(GROUPS):
             for t in range(STRIPE):
                 if sweep == 0:
                     loads[1 + g * STRIPE + t].wait()
-                own[g, :, t * width : (t + 1) * width] = jnp.dot(
+                patch_out[sweep, g, :, t * width : (t + 1) * width] = jnp.dot(
                     turned, basis[:, columns(g, t)], preferred_element_type=F32
-                )
-            mate_out[sweep, g] = own[g, give_at, :].astype(BF16)
+                ).astype(BF16)
             if sweep == 0 and g == 0:
                 pl.semaphore_wait(barrier, len(peers))
                 pass_on(2)
-            copy = remote(mate_out.at[sweep, g], mate_in.at[sweep, g], mate_s.at[sweep, g], mate_r.at[sweep, g], mate)
-            copy.start()
-            mates.append(copy)
-        patch_copies = []
-        for g in range(GROUPS):
-            mates[g].wait_recv()
-            patch_out[sweep, g] = (own[g, keep_at, :] + mate_in[sweep, g].astype(F32)).astype(BF16)
-            copies = []
-            for i, d in enumerate(patch_order):
-                other, other_y, other_stripe = patch_device(d)
+            for h, _, at_y, at_stripe, target in patch:
                 src = patch_out.at[
-                    sweep, g,
-                    pl.ds(pl.multiple_of(other_y * piece_rows, piece_rows), piece_rows),
-                    pl.ds(pl.multiple_of(other_stripe * width, width), width),
+                    sweep, g, piece_at(h, at_y), pl.ds(pl.multiple_of(at_stripe * width, width), width)
                 ]
-                copy = remote(
-                    src, patch_in.at[sweep, g, owner], patch_s.at[sweep, g], patch_r.at[sweep, g], same_half(d)
-                )
-                copy.start()
-                copies.append(copy)
-            patch_in[sweep, g, owner] = patch_out[sweep, g, piece_at, own_width]
-            patch_copies.append(copies)
+                remote(
+                    src, patch_in.at[sweep, g, spot], patch_s.at[sweep, g], patch_r.at[sweep, g], target
+                ).start()
+            patch_in[sweep, g, spot] = patch_out[sweep, g, piece_at(half, y), own_width]
         if sweep == 0:
             pass_on(3)
         far_copies = []
         for g in range(GROUPS):
             if sweep == 0 and g == 0:
                 pass_on(4)
-            settle(meter, len(patch_order), patch_r.at[sweep, g])
+            settle(meter, len(patch), patch_r.at[sweep, g])
             total = patch_in[sweep, g, 0].astype(F32)
-            for j in range(1, owners):
+            for j in range(1, spots):
                 total = total + patch_in[sweep, g, j].astype(F32)
             far_out[sweep, g] = total.astype(BF16)
             if sweep == 0 and g == 0:
@@ -252,7 +241,6 @@
                 copies.append(copy)
             far_in[sweep, g, pair] = far_out[sweep, g]
             far_copies.append(copies)
-        gathers = []
         for g in range(GROUPS):
             settle(meter, len(far_order), far_r.at[sweep, g])
             total = far_in[sweep, g, 0].astype(F32)
@@ -260,20 +248,12 @@
                 total = total + far_in[sweep, g, j].astype(F32)
             mine = coef.at[
                 sweep,
-                pl.ds(pl.multiple_of(half * side + y * piece_rows, piece_rows), piece_rows),
+                piece_at(half, y),
                 pl.ds(pl.multiple_of(stripe * piece_cols + g * width, width), width),
             ]
             mine[...] = (total / m_total).astype(BF16)
-            targets = [mate]
-            for d in patch_order:
-                targets += [same_half(d), other_half(d)]
-            targets = targets[1:] + targets[:1]
-            copies = []
-            for i, target in enumerate(targets):
-                copy = remote(mine, mine, gather_s.at[sweep, g], gather_r.at[sweep, g], target)
-                copy.start()
-                copies.append(copy)
-            gathers.append(copies)
+            for *_, target in patch:
+                remote(mine, mine, gather_s.at[sweep, g], gather_r.at[sweep, g], target).start()
 
         def image_part(rows_at, g):
             out = None
@@ -286,7 +266,7 @@
             return out
 
         for g in range(GROUPS):
-            settle(meter, len(gathers[g]), gather_r.at[sweep, g])
+            settle(meter, len(patch), gather_r.at[sweep, g])
             if g < GROUPS - 1:
                 for c in range(ROW_CHUNKS):
                     part = pl.ds(c * chunk, chunk)
@@ -318,60 +298,35 @@
             left = remainder[part, :] - projected
             remainder[part, :] = left
             low[part, :] = left.astype(BF16)
-        for g in range(GROUPS):
-            mates[g].wait_send()
-            settle(meter, len(patch_order), patch_s.at[sweep, g])
-            settle(meter, len(far_order), far_s.at[sweep, g])
-            settle(meter, len(gathers[g]), gather_s.at[sweep, g])
-        if user_order:
-            gone = image.at[sweep, pl.ds(0, len(user_order)), :, :]
-            pltpu.make_async_copy(gone, gone, users_s.at[sweep]).wait()
 
     loads[-1].wait()
     turned = low[...].astype(F32).T.astype(BF16)
     gown[:, :atoms_b] = jnp.dot(turned, low[...], preferred_element_type=F32)
     gown[:, atoms_b:] = jnp.dot(turned, users[...], preferred_element_type=F32)
-    gram_out[...] = gown[pl.ds(pl.multiple_of((1 - half) * side, side), side), :]
-    copy = remote(gram_out, gram_in, gmate_s.at[0], gmate_r.at[0], mate)
-    copy.start()
-    mate_copy = copy
-    copy.wait_recv()
-    gpatch_out[...] = gown[pl.ds(pl.multiple_of(half * side, side), side), :] + gram_in[...]
-    patch_copies = []
-    for i, d in enumerate(patch_order):
-        other, _, _ = patch_device(d)
-        src = gpatch_out.at[pl.ds(pl.multiple_of(other * gram_rows, gram_rows), gram_rows), :]
-        copy = remote(src, gpatch_in.at[owner], gpatch_s.at[0], gpatch_r.at[0], same_half(d))
-        copy.start()
-        patch_copies.append(copy)
-    gpatch_in[owner] = gpatch_out[pl.ds(pl.multiple_of(owner * gram_rows, gram_rows), gram_rows), :]
-    settle(gmeter, len(patch_copies), gpatch_r.at[0])
+
+    def gram_at(h, at_owner):
+        return pl.ds(pl.multiple_of(h * side + at_owner * gram_rows, gram_rows), gram_rows)
+
+    for h, other, _, _, target in patch:
+        remote(gown.at[gram_at(h, other), :], gpatch_in.at[spot], gpatch_s.at[0], gpatch_r.at[0], target).start()
+    gpatch_in[spot] = gown[gram_at(half, owner), :]
+    settle(gmeter, len(patch), gpatch_r.at[0])
     total = gpatch_in[0]
-    for j in range(1, owners):
+    for j in range(1, spots):
         total = total + gpatch_in[j]
     gpiece[...] = total
-    far_copies = []
-    for i, d in enumerate(far_order):
-        copy = remote(gpiece, gfar_in.at[pair], gfar_s.at[0], gfar_r.at[0], far_device(d))
-        copy.start()
-        far_copies.append(copy)
+    for d in far_order:
+        remote(gpiece, gfar_in.at[pair], gfar_s.at[0], gfar_r.at[0], far_device(d)).start()
     gfar_in[pair] = gpiece[...]
-    settle(gmeter, len(far_copies), gfar_r.at[0])
+    settle(gmeter, len(far_order), gfar_r.at[0])
     total = gfar_in[0]
     for j in range(1, pairs):
         total = total + gfar_in[j]
-    mine = sums.at[pl.ds(pl.multiple_of(half * side + owner * gram_rows, gram_rows), gram_rows), :]
+    mine = sums.at[gram_at(half, owner), :]
     mine[...] = total / m_total
-    gathers = []
-    for i, d in enumerate(patch_order):
-        for j, target in enumerate((same_half(d), other_half(d))):
-            copy = remote(mine, mine, ggather_s.at[0], ggather_r.at[0], target)
-            copy.start()
-            gathers.append(copy)
-    copy = remote(mine, mine, ggather_s.at[0], ggather_r.at[0], mate)
-    copy.start()
-    gathers.append(copy)
-    settle(gmeter, len(gathers), ggather_r.at[0])
+    for *_, target in patch:
+        remote(mine, mine, ggather_s.at[0], ggather_r.at[0], target).start()
+    settle(gmeter, len(patch), ggather_r.at[0])
     factor[...] = sums[:, :atoms_b]
     inverse_factor(factor, spread, atoms_b)
     lines = lax.broadcasted_iota(jnp.int32, (atoms_b, atoms_b), 0)
@@ -380,17 +335,28 @@
     weights = jnp.dot(
         inverse, sums[:, atoms_b:], precision=lax.Precision.HIGHEST, preferred_element_type=F32
     ).astype(BF16)
-    new_block = lax.dot_general(
-        low[...].astype(F32), inverse, (((1,), (1,)), ((), ())),
-        precision=lax.Precision.HIGHEST, preferred_element_type=F32,
-    ).astype(BF16)
-    block_out[...] = new_block
+    turned_inverse = inverse.T
+    high = turned_inverse.astype(BF16)
+    middle = (turned_inverse - high.astype(F32)).astype(BF16)
+    rest = (turned_inverse - high.astype(F32) - middle.astype(F32)).astype(BF16)
+    twice = jnp.concatenate([low[...], low[...]], axis=1)
+    small = jnp.dot(twice, jnp.concatenate([middle, rest], axis=0), preferred_element_type=F32)
+    new_block = (small + jnp.dot(low[...], high, preferred_element_type=F32)).astype(BF16)
+    both_out[:rows, :] = new_block
     updated = users[...].astype(F32) - jnp.dot(new_block, weights, preferred_element_type=F32)
-    updated_out[...] = updated.astype(BF16)
-    mate_copy.wait_send()
-    settle(gmeter, len(patch_copies), gpatch_s.at[0])
-    settle(gmeter, len(far_copies), gfar_s.at[0])
-    settle(gmeter, len(gathers), ggather_s.at[0])
+    both_out[rows:, :] = updated.astype(BF16)
+
+    for sweep in range(2):
+        for g in range(GROUPS):
+            settle(meter, len(patch), patch_s.at[sweep, g])
+            settle(meter, len(far_order), far_s.at[sweep, g])
+            settle(meter, len(patch), gather_s.at[sweep, g])
+        if user_order:
+            gone = image.at[sweep, pl.ds(0, len(user_order)), :, :]
+            pltpu.make_async_copy(gone, gone, users_s.at[sweep]).wait()
+    settle(gmeter, len(patch), gpatch_s.at[0])
+    settle(gmeter, len(far_order), gfar_s.at[0])
+    settle(gmeter, len(patch), ggather_s.at[0])
 
 
 def exchange(old_basis, new_atoms, user_residuals, m_total):
@@ -409,13 +375,10 @@
         pltpu.VMEM((rows, u), BF16),
         pltpu.VMEM((rows, b), BF16),
         pltpu.VMEM((rows, b), F32),
-        pltpu.VMEM((2, GROUPS, side, STRIPE * width), BF16),
-        pltpu.VMEM((2, GROUPS, side, STRIPE * width), BF16),
-        pltpu.VMEM((2, GROUPS, side, STRIPE * width), BF16),
-        pltpu.VMEM((2, GROUPS, owners, *piece), BF16),
+        pltpu.VMEM((2, GROUPS, b, STRIPE * width), BF16),
+        pltpu.VMEM((2, GROUPS, 2 * owners, *piece), BF16),
         pltpu.VMEM((2, GROUPS, *piece), BF16),
         pltpu.VMEM((2, GROUPS, pairs, *piece), BF16),
-        pltpu.VMEM((GROUPS, b, STRIPE * width), F32),
         pltpu.VMEM((2, b, k_loc), BF16),
         pltpu.VMEM((2, X, rows, b), BF16),
         pltpu.VMEM((2, rows, b), BF16),
@@ -425,31 +388,30 @@
         pltpu.VMEM((b, b + u), F32),
         pltpu.VMEM((b, b), F32),
         pltpu.VMEM((STEP * STEP, b), F32),
-        pltpu.VMEM((side, b + u), F32),
-        pltpu.VMEM((side, b + u), F32),
-        pltpu.VMEM((side, b + u), F32),
-        pltpu.VMEM((owners, *gram_piece), F32),
+        pltpu.VMEM((2 * owners, *gram_piece), F32),
         pltpu.VMEM((pairs, *gram_piece), F32),
         pltpu.VMEM((b, b + u), F32),
         pltpu.VMEM(gram_piece, F32),
         dma((2 + GROUPS * STRIPE,)), signal((3,)), signal((2,)),
-        *[dma((2, GROUPS))] * 8,
+        *[dma((2, GROUPS))] * 6,
         dma((2,)), dma((2, ROW_CHUNKS)),
-        *[dma((1,))] * 8,
+        *[dma((1,))] * 6,
     ]
     return pl.pallas_call(
         functools.partial(exchange_kernel, m_total),
-        out_shape=(jax.ShapeDtypeStruct((rows, b), BF16), jax.ShapeDtypeStruct((rows, u), BF16)),
+        out_shape=jax.ShapeDtypeStruct((2 * rows, b), BF16),
         in_specs=[pl.BlockSpec(memory_space=pl.ANY)] * 3,
-        out_specs=(pl.BlockSpec(memory_space=pltpu.VMEM), pl.BlockSpec(memory_space=pltpu.VMEM)),
+        out_specs=pl.BlockSpec(memory_space=pltpu.VMEM),
         scratch_shapes=scratch,
-        compiler_params=pltpu.CompilerParams(collective_id=0, has_side_effects=True, vmem_limit_bytes=55000 * 1024),
-    )(old_basis, new_atoms, user_residuals)
+        compiler_params=pltpu.CompilerParams(collective_id=0, has_side_effects=True, vmem_limit_bytes=48 * 2**20),
+    )(*(pltpu.with_memory_space_constraint(v, pltpu.HBM) for v in (old_basis, new_atoms, user_residuals)))
 
 
 def local(old_basis, new_atoms, user_residuals):
     m_total = float(old_basis.shape[0] * lax.axis_size("rows"))
-    return exchange(old_basis, new_atoms, user_residuals, m_total)
+    both = exchange(old_basis, new_atoms, user_residuals, m_total)
+    rows = old_basis.shape[0]
+    return both[:rows], both[rows:]
 
 
 def solution(mesh):

time: 91.8 us -> 90.7 us (0.988)
    unnamed x2 -> x0, local copies, waits for them, and re-layouts: 1.28 us -> none
where the time goes in v5:
time: 90.7 us; the launch traced here: 90.6 us
  Pallas kernels  89.3 us (98%)
    pallas_call x1, Pallas kernels, exchange(): pl.pallas_call(functools.partial(exchange_kernel, m_total), out_shape=jax...  89.3 us

profile of v5, /device:TPU:1, one launch (start us, length us, event | category | flops | bytes accessed | tf_op | source)
XLA Modules:
  0.0 90.6 jit_solution(2123566615241919101)
XLA Ops:
  0.6 89.3 %shard_map.50 = bf16[768,128]{1,0:T(8,128)(2,1)S(1)} custom-call(bf16[384,1024]{1,0:T(8,128)(2,1)} %basis_hbm.1, bf16[384,128]{1,0:T(8,128)(2,1)} %atoms_hbm.1, bf16[384,128]{1,0:T(8,128)(2,1)} %users_hbm.1), custom_call_target="tpu_custom_call" | custom-call | tf_op jit(solution)/shard_map/pallas_call | solution.py:400
  89.9 0.7 fusion
